TPU v7x, 256 devices: a whole 4x4x8 slice. The times are simulated.
256 devices in a mesh: dom: 32 (over x, z), load: 8 (over y, core).
Axes of the slice: x: 4, y: 4, z: 8, core: 2. Of those that a mesh axis runs over, the one named last changes fastest.
Arguments:
- load_current: float32 [8, 49152], P('load', 'dom'), may hold values from 0.1 to 1
- worst_node: int32 [8], P('load'), may hold values from 0 to 49151
- cond_diag: float32 [49152], P('dom'), may hold values from 0.5 to 4
- branch: float32 [384, 128, 128], P('dom'), may hold values from -0.5 to 0.5
- precond_factor: float32 [384, 128, 128], P('dom'), may hold values from -0.5 to 0.5
- coupling: float32 [5, 384, 128, 128], P(None, 'dom'), may hold values from -0.5 to 0.5
- sep_map: int32 [5, 384], P(None, 'dom'), may hold values from 0 to 11
- strap_ends: int32 [2, 524288], P(None, 'dom'), may hold values from 0 to 1535
Outputs:
- voltages: float32 [2, 8, 49152], P(None, 'load', 'dom')
- strap_grad: float32 [524288], P('dom')
Inputs may be any that keep to these rules, and one draw needn't show every extreme that they name: `sep_map`: each entry names an interior block of the same partition as the separator block. `strap_ends`: both ends of a strap lie in the partition that holds the strap. `worst_node`: a global node index.
All inputs are finite; a program needn't handle non-finite values.
Results may differ from a plain program's by a relative error of at most 0.00017.
Values sent between devices are 32-bit elements; how exact they have to be, the bound alone decides.
No kernel may reach another device: no remote copies, remote signals or barrier semaphores. Data moves between devices by JAX's collectives and lax.ppermute only.
A program may use at most 128 MiB of HBM per device.

v0:
```python
import math
import jax
import jax.numpy as jnp
from jax import lax
from jax.sharding import PartitionSpec as P

ITERS = 4
HIGHEST = lax.Precision.HIGHEST


def swapped(value, axis, apart):
    mask = 2**apart
    pairs = [(source, source ^ mask) for source in range(lax.axis_size(axis))]
    return lax.ppermute(value, axis, pairs)


def subtree_sums(contrib):
    levels = contrib.shape[0]
    finished = []
    pending = contrib
    for level_no in range(levels):
        pending = pending + swapped(pending, "dom", level_no)
        finished.append(pending[0])
        pending = pending[1:]
    return jnp.stack(finished)


def coarse_part(blocks, coupling, picker, level_weights):
    selected = jnp.einsum("ljb,rbn->lrjn", picker, blocks, precision=HIGHEST)
    contrib = jnp.einsum("ljmn,lrjn->lrjm", coupling, selected, precision=HIGHEST)
    group_sums = subtree_sums(contrib)
    returned = jnp.einsum("ljmn,lrjm->lrjn", coupling, group_sums, precision=HIGHEST)
    weighted = picker * level_weights[:, None, None]
    return jnp.einsum("ljb,lrjn->rbn", weighted, returned, precision=HIGHEST)


def factor_apply(factor, blocks):
    inner = jnp.einsum("jnk,rjn->rjk", factor, blocks, precision=HIGHEST)
    return jnp.einsum("jnk,rjk->rjn", factor, inner, precision=HIGHEST)


def column_sums(first, second):
    return lax.psum(jnp.sum(first * second, axis=(1, 2)), "dom")


def shards(
    load_current, worst_node, cond_diag, branch, precond_factor, coupling, sep_map, strap_ends
):
    levels = coupling.shape[0]
    nblocks = branch.shape[0]
    width = branch.shape[1]
    node_count = nblocks * width
    time_count = load_current.shape[0]
    shunt = cond_diag.reshape(nblocks, width)
    picker = (sep_map[:, :, None] == jnp.arange(nblocks, dtype=jnp.int32)[None, None, :]).astype(
        jnp.float32
    )
    op_weights = jnp.array(
        [1.0 / math.sqrt(2.0 ** (level_no + 1)) for level_no in range(levels)], jnp.float32
    )
    pre_weights = 0.5 * op_weights
    node_ids = lax.axis_index("dom") * node_count + jnp.arange(node_count, dtype=jnp.int32)
    adjoint_rhs = (node_ids[None, :] == worst_node[:, None]).astype(jnp.float32)
    sources = jnp.concatenate([load_current, adjoint_rhs], 0).reshape(
        2 * time_count, nblocks, width
    )

    def apply_precond(blocks):
        return (
            blocks / (shunt + 1.0)
            + 0.25 * factor_apply(precond_factor, blocks)
            + coarse_part(blocks, coupling, picker, pre_weights)
        )

    solution = jnp.zeros_like(sources)
    residual = sources
    precond_res = apply_precond(residual)
    rho_now = column_sums(residual, precond_res)
    direction = precond_res
    for iteration in range(ITERS):
        mapped = (
            shunt * direction
            + factor_apply(branch, direction)
            + coarse_part(direction, coupling, picker, op_weights)
        )
        step_size = rho_now / column_sums(direction, mapped)
        solution = solution + step_size[:, None, None] * direction
        residual = residual - step_size[:, None, None] * mapped
        if iteration + 1 < ITERS:
            precond_res = apply_precond(residual)
            rho_new = column_sums(residual, precond_res)
            direction = precond_res + (rho_new / rho_now)[:, None, None] * direction
            rho_now = rho_new
    voltages = solution.reshape(2, time_count, node_count)
    forward = voltages[0]
    adjoint = voltages[1]
    drop_diff = forward[:, strap_ends[0]] - forward[:, strap_ends[1]]
    adj_diff = adjoint[:, strap_ends[0]] - adjoint[:, strap_ends[1]]
    strap_grad = lax.psum(-jnp.sum(adj_diff * drop_diff, axis=0), "load")
    return (voltages, strap_grad)


def solution(mesh):
    placed = (
        P("load", "dom"),
        P("load"),
        P("dom"),
        P("dom", None, None),
        P("dom", None, None),
        P(None, "dom", None, None),
        P(None, "dom"),
        P(None, "dom"),
    )
    return jax.shard_map(
        shards,
        mesh=mesh,
        in_specs=placed,
        out_specs=(P(None, "load", "dom"), P("dom")),
        check_vma=False,
    )
```

profile of v0, /device:TPU:2, one launch (start us, length us, event | category | flops | bytes accessed | tf_op | source)
XLA Modules:
  0.0 1265.0 jit_solution(7190926894018627140)
XLA Ops:
  10.0 7.9 convolution_bitcast_fusion.7
  22.2 3.4 collective-permute-start.1
  27.7 7.0 collective-permute-start.2
  42.9 3.1 collective-permute-done.4
  46.0 3.4 fusion.144
  51.4 6.2 convolution_bitcast_fusion.6
  58.7 3.2 collective-permute-done.5
  64.0 3.1 collective-permute-done.6
  67.1 6.9 collective-permute-start.7
  79.9 2.8 collective-permute-start.9
  85.5 3.4 fusion.145
  90.7 64.4 %all-reduce = (f32[2]{0:T(128)S(1)}, f32[2]{0:T(128)S(1)}) all-reduce(f32[2]{0:T(128)S(1)} %get-tuple-element.7, f32[2]{0:T(128)S(1)} %get-tuple-element.6), channel_id=1, replica_groups=mesh['dom'=32,'load'=8] {'dom'}, use_global_device_ids=true, to_apply=%region_1.0 | all-reduce | flops 4 | bytes 32 | tf_op jit(solution)/shard_map/psum | solution.py:43
  155.5 8.0 convolution_bitcast_fusion.5
  163.6 4.2 collective-permute-done.10
  167.9 5.0 collective-permute-done.11
  173.1 7.8 collective-permute-done.12
  180.9 12.3 collective-permute-start.13
  196.4 4.4 collective-permute-done.14
  200.8 3.4 fusion.146
  206.0 60.2 %psum.65 = f32[2]{0:T(128)S(1)} all-reduce(f32[2]{0:T(128)S(1)} %get-tuple-element.29), channel_id=1, replica_groups=mesh['dom'=32,'load'=8] {'dom'}, use_global_device_ids=true, to_apply=%region_5.0 | all-reduce | flops 2 | bytes 16 | tf_op jit(solution)/shard_map/psum | solution.py:43
  266.6 8.0 convolution_bitcast_fusion.4
  276.4 2.4 collective-permute-done.15
  279.0 5.0 collective-permute-done.16
  284.2 7.8 collective-permute-done.17
  292.1 11.9 collective-permute-start.18
  306.9 4.4 collective-permute-done.19
  311.3 3.4 fusion.147
  316.5 62.2 %psum.66 = f32[2]{0:T(128)S(1)} all-reduce(f32[2]{0:T(128)S(1)} %get-tuple-element.31), channel_id=1, replica_groups=mesh['dom'=32,'load'=8] {'dom'}, use_global_device_ids=true, to_apply=%region_7.0 | all-reduce | flops 2 | bytes 16 | tf_op jit(solution)/shard_map/psum | solution.py:43
  379.1 8.0 convolution_bitcast_fusion.3
  387.2 4.2 collective-permute-done.20
  391.6 5.0 collective-permute-done.21
  396.8 7.9 collective-permute-done.22
  404.7 11.7 collective-permute-start.23
  419.3 4.4 collective-permute-done.24
  423.8 3.4 fusion.148
  429.0 60.2 %psum.67 = f32[2]{0:T(128)S(1)} all-reduce(f32[2]{0:T(128)S(1)} %get-tuple-element.33), channel_id=1, replica_groups=mesh['dom'=32,'load'=8] {'dom'}, use_global_device_ids=true, to_apply=%region_9.0 | all-reduce | flops 2 | bytes 16 | tf_op jit(solution)/shard_map/psum | solution.py:43
  489.5 8.0 convolution_bitcast_fusion.2
  499.3 2.5 collective-permute-done.25
  502.0 5.0 collective-permute-done.26
  507.1 7.8 collective-permute-done.27
  515.0 12.2 collective-permute-start.28
  530.3 4.4 collective-permute-done.29
  534.7 3.4 fusion.149
  539.9 61.7 %psum.68 = f32[2]{0:T(128)S(1)} all-reduce(f32[2]{0:T(128)S(1)} %get-tuple-element.35), channel_id=1, replica_groups=mesh['dom'=32,'load'=8] {'dom'}, use_global_device_ids=true, to_apply=%region_11.0 | all-reduce | flops 2 | bytes 16 | tf_op jit(solution)/shard_map/psum | solution.py:43
  601.9 8.0 convolution_bitcast_fusion.1
  610.3 3.9 collective-permute-done.30
  614.4 5.2 collective-permute-done.31
  619.8 7.8 collective-permute-done.32
  627.7 11.7 collective-permute-start.33
  642.3 4.4 collective-permute-done.34
  646.8 3.4 fusion.150
  652.0 60.2 %psum.69 = f32[2]{0:T(128)S(1)} all-reduce(f32[2]{0:T(128)S(1)} %get-tuple-element.37), channel_id=1, replica_groups=mesh['dom'=32,'load'=8] {'dom'}, use_global_device_ids=true, to_apply=%region_13.0 | all-reduce | flops 2 | bytes 16 | tf_op jit(solution)/shard_map/psum | solution.py:43
  712.5 8.0 convolution_bitcast_fusion
  725.0 5.0 collective-permute-done.36
  730.1 7.8 collective-permute-done.37
  738.0 11.8 collective-permute-start.38
  752.7 4.4 collective-permute-done.39
  757.1 3.4 fusion.151
  762.4 62.0 %psum.70 = f32[2]{0:T(128)S(1)} all-reduce(f32[2]{0:T(128)S(1)} %fusion.21), channel_id=1, replica_groups=mesh['dom'=32,'load'=8] {'dom'}, use_global_device_ids=true, to_apply=%region_15.0 | all-reduce | flops 2 | bytes 16 | tf_op jit(solution)/shard_map/psum | solution.py:43
  824.5 90.5 %gather_fusion.3 = f32[16384]{0:T(1024)S(1)} fusion(f32[1536]{0:T(1024)S(1)} %bitcast.279, s32[16384]{0:T(1024)S(1)} %get-tuple-element.39), kind=kCustom, calls=%fused_computation.3 | custom fusion | bytes 196608 | tf_op jit(solution)/shard_map/gather | solution.py:97
  915.0 90.5 %gather_fusion.1 = f32[16384]{0:T(1024)S(1)} fusion(f32[1536]{0:T(1024)S(1)} %bitcast.281, s32[16384]{0:T(1024)S(1)} %get-tuple-element.39), kind=kCustom, calls=%fused_computation.1 | custom fusion | bytes 196608 | tf_op jit(solution)/shard_map/gather | solution.py:98
  1005.6 90.5 %gather_fusion = f32[16384]{0:T(1024)S(1)} fusion(f32[1536]{0:T(1024)S(1)} %bitcast.282, s32[16384]{0:T(1024)S(1)} %get-tuple-element.40), kind=kCustom, calls=%fused_computation | custom fusion | bytes 196608 | tf_op jit(solution)/shard_map/gather | solution.py:98
  1096.1 90.5 %gather_fusion.2 = f32[16384]{0:T(1024)S(1)} fusion(f32[1536]{0:T(1024)S(1)} %bitcast.280, s32[16384]{0:T(1024)S(1)} %get-tuple-element.40), kind=kCustom, calls=%fused_computation.2 | custom fusion | bytes 196608 | tf_op jit(solution)/shard_map/gather | solution.py:97
  1188.0 68.5 %all-reduce.3.cloned.1.call-done = f32[16384]{0:T(1024)} async-done(((f32[16384]{0:T(1024)}), f32[16384]{0:T(1024)}) %all-reduce.3.cloned.1.call-update) | async-done | bytes 65552 | tf_op jit(solution)/shard_map/psum | solution.py:99
  (227 shorter events, 75.7 us)
Async XLA Ops:
  7.2 12.7 %copy-start = (f32[12,128,128]{2,1,0:T(8,128)S(1)}, f32[12,128,128]{2,1,0:T(8,128)}, u32[]{:S(2)}) copy-start(f32[12,128,128]{2,1,0:T(8,128)} %param.13) | copy-start | bytes 2359300
  7.2 12.7 %copy-start.10 = (f32[1,1536]{1,0:T(1,128)S(1)}, f32[1,1536]{1,0:T(1,128)}, u32[]{:S(2)}) copy-start(f32[1,1536]{1,0:T(1,128)} %param.9) | copy-start | bytes 18436
  7.2 35.8 %copy-start.11 = (f32[1536]{0:T(1024)S(1)}, f32[1536]{0:T(1024)}, u32[]{:S(2)}) copy-start(f32[1536]{0:T(1024)} %param.11) | copy-start | bytes 18436
  7.2 1249.2 %all-reduce.3.cloned.1.call-start = ((), (), s32[]{:S(2)}) async-start(), calls=%async_computation | async-start | bytes 131072 | tf_op jit(solution)/shard_map/psum | solution.py:99
  8.0 38.1 %copy-start.1 = (f32[5,12,128,128]{3,2,1,0:T(8,128)S(1)}, f32[5,12,128,128]{3,2,1,0:T(8,128)}, u32[]{:S(2)}) copy-start(f32[5,12,128,128]{3,2,1,0:T(8,128)} %param.14) | copy-start | bytes 11796484
  10.0 39.5 %copy-start.9 = (s32[5,12]{1,0:T(8,128)S(1)}, s32[5,12]{1,0:T(8,128)}, u32[]{:S(2)}) copy-start(s32[5,12]{1,0:T(8,128)} %param.15) | copy-start | bytes 724
  10.0 39.5 %copy-start.14 = (f32[5]{0:T(128)S(1)}, f32[5]{0:T(128)}, u32[]{:S(2)}) copy-start(f32[5]{0:T(128)} %constant.32) | copy-start | bytes 64
  17.9 4.3 collective-permute-start
  22.2 5.4 collective-permute-start.1
  27.7 8.9 collective-permute-start.2
  36.6 3.9 collective-permute-start.3
  40.6 5.5 collective-permute-start.4
  49.5 33.2 %copy-start.8 = (f32[12,128,128]{2,1,0:T(8,128)S(1)}, f32[12,128,128]{2,1,0:T(8,128)}, u32[]{:S(2)}) copy-start(f32[12,128,128]{2,1,0:T(8,128)} %param.12) | copy-start | bytes 2359300
  51.4 37.5 %copy-start.13 = (f32[5]{0:T(128)S(1)}, f32[5]{0:T(128)}, u32[]{:S(2)}) copy-start(f32[5]{0:T(128)} %constant.25.clone) | copy-start | bytes 64
  57.6 4.2 collective-permute-start.5
  61.9 5.1 collective-permute-start.6
  67.1 8.9 collective-permute-start.7
  76.0 3.9 collective-permute-start.8
  79.9 5.5 collective-permute-start.9
  155.1 45.7 %copy-start.2 = (f32[5,12,128,128]{3,2,1,0:T(8,128)S(1)}, f32[5,12,128,128]{3,2,1,0:T(8,128)}, u32[]{:S(2)}) copy-start(f32[5,12,128,128]{3,2,1,0:T(8,128)} %param.14) | copy-start | bytes 11796484
  163.5 4.3 collective-permute-start.10
  167.8 5.1 collective-permute-start.11
  173.0 8.0 collective-permute-start.12
  180.9 14.1 %collective-permute-start.13 = (f32[2,2,12,128]{3,1,2,0:T(2,128)S(1)}, f32[2,2,12,128]{3,1,2,0:T(2,128)S(1)}, u32[]{:S(2)}, u32[]{:S(2)}) collective-permute-start(f32[2,2,12,128]{3,1,2,0:T(2,128)S(1)} %slice.305), channel_id=1, source_target_pairs={{0,64},{8,72},{16,80},{24,88},{32,96},{40,104},{48,112},{56,120},{... | collective-permute-start | bytes 73736 | tf_op jit(solution)/shard_map/ppermute | solution.py:14
  195.1 5.7 collective-permute-start.14
  266.2 45.1 %copy-start.3 = (f32[5,12,128,128]{3,2,1,0:T(8,128)S(1)}, f32[5,12,128,128]{3,2,1,0:T(8,128)}, u32[]{:S(2)}) copy-start(f32[5,12,128,128]{3,2,1,0:T(8,128)} %param.14) | copy-start | bytes 11796484
  274.6 4.3 collective-permute-start.15
  278.9 5.1 collective-permute-start.16
  284.1 8.0 collective-permute-start.17
  292.1 13.7 %collective-permute-start.18 = (f32[2,2,12,128]{3,1,2,0:T(2,128)S(1)}, f32[2,2,12,128]{3,1,2,0:T(2,128)S(1)}, u32[]{:S(2)}, u32[]{:S(2)}) collective-permute-start(f32[2,2,12,128]{3,1,2,0:T(2,128)S(1)} %slice.313), channel_id=1, source_target_pairs={{0,64},{8,72},{16,80},{24,88},{32,96},{40,104},{48,112},{56,120},{... | collective-permute-start | bytes 73736 | tf_op jit(solution)/shard_map/ppermute | solution.py:14
  305.9 5.5 collective-permute-start.19
  378.8 45.0 %copy-start.4 = (f32[5,12,128,128]{3,2,1,0:T(8,128)S(1)}, f32[5,12,128,128]{3,2,1,0:T(8,128)}, u32[]{:S(2)}) copy-start(f32[5,12,128,128]{3,2,1,0:T(8,128)} %param.14) | copy-start | bytes 11796484
  387.2 4.3 collective-permute-start.20
  391.5 5.1 collective-permute-start.21
  396.7 8.0 collective-permute-start.22
  404.7 13.5 %collective-permute-start.23 = (f32[2,2,12,128]{3,1,2,0:T(2,128)S(1)}, f32[2,2,12,128]{3,1,2,0:T(2,128)S(1)}, u32[]{:S(2)}, u32[]{:S(2)}) collective-permute-start(f32[2,2,12,128]{3,1,2,0:T(2,128)S(1)} %slice.321), channel_id=1, source_target_pairs={{0,64},{8,72},{16,80},{24,88},{32,96},{40,104},{48,112},{56,120},{... | collective-permute-start | bytes 73736 | tf_op jit(solution)/shard_map/ppermute | solution.py:14
  418.2 5.5 collective-permute-start.24
  489.2 45.5 %copy-start.5 = (f32[5,12,128,128]{3,2,1,0:T(8,128)S(1)}, f32[5,12,128,128]{3,2,1,0:T(8,128)}, u32[]{:S(2)}) copy-start(f32[5,12,128,128]{3,2,1,0:T(8,128)} %param.14) | copy-start | bytes 11796484
  497.5 4.3 collective-permute-start.25
  501.9 5.1 collective-permute-start.26
  507.0 8.0 collective-permute-start.27
  515.0 14.0 %collective-permute-start.28 = (f32[2,2,12,128]{3,1,2,0:T(2,128)S(1)}, f32[2,2,12,128]{3,1,2,0:T(2,128)S(1)}, u32[]{:S(2)}, u32[]{:S(2)}) collective-permute-start(f32[2,2,12,128]{3,1,2,0:T(2,128)S(1)} %slice.329), channel_id=1, source_target_pairs={{0,64},{8,72},{16,80},{24,88},{32,96},{40,104},{48,112},{56,120},{... | collective-permute-start | bytes 73736 | tf_op jit(solution)/shard_map/ppermute | solution.py:14
  529.0 5.7 collective-permute-start.29
  601.6 45.1 %copy-start.6 = (f32[5,12,128,128]{3,2,1,0:T(8,128)S(1)}, f32[5,12,128,128]{3,2,1,0:T(8,128)}, u32[]{:S(2)}) copy-start(f32[5,12,128,128]{3,2,1,0:T(8,128)} %param.14) | copy-start | bytes 11796484
  610.0 4.3 collective-permute-start.30
  614.3 5.4 collective-permute-start.31
  619.7 8.0 collective-permute-start.32
  627.7 13.5 %collective-permute-start.33 = (f32[2,2,12,128]{3,1,2,0:T(2,128)S(1)}, f32[2,2,12,128]{3,1,2,0:T(2,128)S(1)}, u32[]{:S(2)}, u32[]{:S(2)}) collective-permute-start(f32[2,2,12,128]{3,1,2,0:T(2,128)S(1)} %slice.337), channel_id=1, source_target_pairs={{0,64},{8,72},{16,80},{24,88},{32,96},{40,104},{48,112},{56,120},{... | collective-permute-start | bytes 73736 | tf_op jit(solution)/shard_map/ppermute | solution.py:14
  641.3 5.5 collective-permute-start.34
  646.7 75.6 %copy-start.12 = (s32[2,16384]{1,0:T(2,128)S(1)}, s32[2,16384]{1,0:T(2,128)}, u32[]{:S(2)}) copy-start(s32[2,16384]{1,0:T(2,128)} %param.16) | copy-start | bytes 393220
  712.2 44.9 %copy-start.7 = (f32[5,12,128,128]{3,2,1,0:T(8,128)S(1)}, f32[5,12,128,128]{3,2,1,0:T(8,128)}, u32[]{:S(2)}) copy-start(f32[5,12,128,128]{3,2,1,0:T(8,128)} %param.14) | copy-start | bytes 11796484
  720.6 4.3 collective-permute-start.35
  724.9 5.1 collective-permute-start.36
  730.0 8.0 collective-permute-start.37
  738.0 13.6 %collective-permute-start.38 = (f32[2,2,12,128]{3,1,2,0:T(2,128)S(1)}, f32[2,2,12,128]{3,1,2,0:T(2,128)S(1)}, u32[]{:S(2)}, u32[]{:S(2)}) collective-permute-start(f32[2,2,12,128]{3,1,2,0:T(2,128)S(1)} %slice.345), channel_id=1, source_target_pairs={{0,64},{8,72},{16,80},{24,88},{32,96},{40,104},{48,112},{56,120},{... | collective-permute-start | bytes 73736 | tf_op jit(solution)/shard_map/ppermute | solution.py:14
  751.6 5.5 collective-permute-start.39
Sparse Core Ops, SparseCore 0:
  1187.5 68.9 all-reduce.2
where the time goes:
time: 1270 us; the launch traced here: 1260 us
  blocking collectives  431 us (34%)
  local copies, waits for them, and re-layouts  365 us (29%)
  waiting for transfers between devices  226 us (18%)
  matrix products  113 us (9%)
  starting transfers between devices  112 us (9%)
  between operations  15.9 us (1%)
    psum x7, blocking collectives, column_sums(): return lax.psum(jnp.sum(first * second, axis=(1, 2)), 'dom')  431 us
    gather x2, local copies, waits for them, and re-layouts, shards(): adj_diff = adjoint[:, strap_ends[0]] - adjoint[:, strap_ends[1]]  181 us
    gather x2, local copies, waits for them, and re-layouts, shards(): drop_diff = forward[:, strap_ends[0]] - forward[:, strap_ends[1]]  181 us
    ppermute x40, waiting for transfers between devices, swapped(): return lax.ppermute(value, axis, pairs)  157 us
    ppermute x40, starting transfers between devices, swapped(): return lax.ppermute(value, axis, pairs)  112 us
    psum x1, waiting for transfers between devices, shards(): strap_grad = lax.psum(-jnp.sum(adj_diff * drop_diff, axis=0), 'load')  68.5 us
    dot_general x8, matrix products, coarse_part(): jnp.einsum('ljmn,lrjn->lrjm', coupling, selected, precision=HIGHEST)  62.3 us
    dot_general x8, matrix products, coarse_part(): jnp.einsum('ljmn,lrjm->lrjn', coupling, group_sums, precision=HIGHEST)  27.5 us
  transfers between devices with their start and end apart: 41, of which 41 were waited for; matrix products, arithmetic and copies ran while one was open for 1% of the time, Pallas kernels for 0%

commit v1 on v0

--- a/solution.py
+++ b/solution.py
@@ -96,7 +96,9 @@
     adjoint = voltages[1]
     drop_diff = forward[:, strap_ends[0]] - forward[:, strap_ends[1]]
     adj_diff = adjoint[:, strap_ends[0]] - adjoint[:, strap_ends[1]]
-    strap_grad = lax.psum(-jnp.sum(adj_diff * drop_diff, axis=0), "load")
+    x = -jnp.sum(adj_diff * drop_diff, axis=0)
+    parts = lax.all_gather(x, "load", axis=0, tiled=False)
+    strap_grad = parts.sum(axis=0)
     return (voltages, strap_grad)
 
 

time: 1270 us -> 1210 us (0.953)
  waiting for transfers between devices: 226 us -> 157 us
  blocking collectives: 431 us -> 445 us
  between operations: 15.9 us -> 2.49 us
    psum x1 -> x0, waiting for transfers between devices: 68.5 us -> none  [shards(): strap_grad = lax.psum(-jnp.sum(adj_diff * drop_diff, axis=0), 'load')]
    all_gather x0 -> x1, blocking collectives: none -> 13.6 us  [shards(): parts = lax.all_gather(x, 'load', axis=0, tiled=False)]
  transfers between devices with their start and end apart: 41 -> 40, of which waited for: 41 -> 40; matrix products, arithmetic and copies ran while one was open for 1% -> 1% of each run, Pallas kernels for 0% -> 0%
where the time goes in v1:
time: 1210 us; the launch traced here: 1200 us
  blocking collectives  445 us (37%)
  local copies, waits for them, and re-layouts  363 us (30%)
  waiting for transfers between devices  157 us (13%)
  matrix products  113 us (9%)
  starting transfers between devices  112 us (9%)
    psum x7, blocking collectives, column_sums(): return lax.psum(jnp.sum(first * second, axis=(1, 2)), 'dom')  431 us
    gather x2, local copies, waits for them, and re-layouts, shards(): drop_diff = forward[:, strap_ends[0]] - forward[:, strap_ends[1]]  181 us
    gather x2, local copies, waits for them, and re-layouts, shards(): adj_diff = adjoint[:, strap_ends[0]] - adjoint[:, strap_ends[1]]  181 us
    ppermute x40, waiting for transfers between devices, swapped(): return lax.ppermute(value, axis, pairs)  157 us
    ppermute x40, starting transfers between devices, swapped(): return lax.ppermute(value, axis, pairs)  112 us
    dot_general x8, matrix products, coarse_part(): jnp.einsum('ljmn,lrjn->lrjm', coupling, selected, precision=HIGHEST)  62.3 us
    dot_general x8, matrix products, coarse_part(): jnp.einsum('ljmn,lrjm->lrjn', coupling, group_sums, precision=HIGHEST)  27.5 us
  transfers between devices with their start and end apart: 40, of which 40 were waited for; matrix products, arithmetic and copies ran while one was open for 1% of the time, Pallas kernels for 0%

profile of v1, /device:TPU:2, one launch (start us, length us, event | category | flops | bytes accessed | tf_op | source)
XLA Modules:
  0.0 1195.4 jit_solution(9342061517297214624)
XLA Ops:
  3.4 7.9 convolution_bitcast_fusion.23
  15.6 3.4 collective-permute-start.1
  21.1 7.0 collective-permute-start.2
  36.4 3.1 collective-permute-done.4
  39.5 3.4 convolution_bitcast_fusion.22
  44.8 6.2 convolution_bitcast_fusion.21
  52.1 3.2 collective-permute-done.5
  57.4 3.1 collective-permute-done.6
  60.5 6.9 collective-permute-start.7
  73.4 2.8 collective-permute-start.9
  78.9 3.4 convolution_bitcast_fusion.20
  84.1 64.4 %all-reduce = (f32[2]{0:T(128)S(1)}, f32[2]{0:T(128)S(1)}) all-reduce(f32[2]{0:T(128)S(1)} %get-tuple-element.11, f32[2]{0:T(128)S(1)} %get-tuple-element.10), channel_id=1, replica_groups=mesh['dom'=32,'load'=8] {'dom'}, use_global_device_ids=true, to_apply=%region_1.0 | all-reduce | flops 4 | bytes 32 | tf_op jit(solution)/shard_map/psum | solution.py:43
  148.9 8.0 convolution_bitcast_fusion.19
  157.0 4.2 collective-permute-done.10
  161.4 5.0 collective-permute-done.11
  166.5 7.8 collective-permute-done.12
  174.4 12.4 %collective-permute-start.13 = (f32[2,2,12,128]{3,1,2,0:T(2,128)S(1)}, f32[2,2,12,128]{3,1,2,0:T(2,128)S(1)}, u32[]{:S(2)}, u32[]{:S(2)}) collective-permute-start(f32[2,2,12,128]{3,1,2,0:T(2,128)S(1)} %slice.305), channel_id=1, source_target_pairs={{0,64},{8,72},{16,80},{24,88},{32,96},{40,104},{48,112},{56,120},{... | collective-permute-start | bytes 73736 | tf_op jit(solution)/shard_map/ppermute | solution.py:14
  189.8 4.4 collective-permute-done.14
  194.3 3.4 convolution_bitcast_fusion.18
  199.5 60.2 %psum.58 = f32[2]{0:T(128)S(1)} all-reduce(f32[2]{0:T(128)S(1)} %get-tuple-element.33), channel_id=1, replica_groups=mesh['dom'=32,'load'=8] {'dom'}, use_global_device_ids=true, to_apply=%region_5.0 | all-reduce | flops 2 | bytes 16 | tf_op jit(solution)/shard_map/psum | solution.py:43
  260.0 8.0 convolution_bitcast_fusion.17
  269.9 2.4 collective-permute-done.15
  272.5 5.0 collective-permute-done.16
  277.6 7.8 collective-permute-done.17
  285.5 11.9 collective-permute-start.18
  300.3 4.4 collective-permute-done.19
  304.8 3.4 convolution_bitcast_fusion.16
  310.0 62.2 %psum.59 = f32[2]{0:T(128)S(1)} all-reduce(f32[2]{0:T(128)S(1)} %get-tuple-element.35), channel_id=1, replica_groups=mesh['dom'=32,'load'=8] {'dom'}, use_global_device_ids=true, to_apply=%region_7.0 | all-reduce | flops 2 | bytes 16 | tf_op jit(solution)/shard_map/psum | solution.py:43
  372.5 8.0 convolution_bitcast_fusion.15
  380.6 4.3 collective-permute-done.20
  385.0 5.0 collective-permute-done.21
  390.2 7.9 collective-permute-done.22
  398.1 11.7 collective-permute-start.23
  412.7 4.4 collective-permute-done.24
  417.2 3.4 convolution_bitcast_fusion.14
  422.4 60.2 %psum.60 = f32[2]{0:T(128)S(1)} all-reduce(f32[2]{0:T(128)S(1)} %get-tuple-element.37), channel_id=1, replica_groups=mesh['dom'=32,'load'=8] {'dom'}, use_global_device_ids=true, to_apply=%region_9.0 | all-reduce | flops 2 | bytes 16 | tf_op jit(solution)/shard_map/psum | solution.py:43
  482.9 8.0 convolution_bitcast_fusion.13
  492.7 2.5 collective-permute-done.25
  495.4 5.0 collective-permute-done.26
  500.5 7.8 collective-permute-done.27
  508.4 12.2 %collective-permute-start.28 = (f32[2,2,12,128]{3,1,2,0:T(2,128)S(1)}, f32[2,2,12,128]{3,1,2,0:T(2,128)S(1)}, u32[]{:S(2)}, u32[]{:S(2)}) collective-permute-start(f32[2,2,12,128]{3,1,2,0:T(2,128)S(1)} %slice.329), channel_id=1, source_target_pairs={{0,64},{8,72},{16,80},{24,88},{32,96},{40,104},{48,112},{56,120},{... | collective-permute-start | bytes 73736 | tf_op jit(solution)/shard_map/ppermute | solution.py:14
  523.7 4.4 collective-permute-done.29
  528.1 3.4 convolution_bitcast_fusion.12
  533.3 61.7 %psum.61 = f32[2]{0:T(128)S(1)} all-reduce(f32[2]{0:T(128)S(1)} %get-tuple-element.39), channel_id=1, replica_groups=mesh['dom'=32,'load'=8] {'dom'}, use_global_device_ids=true, to_apply=%region_11.0 | all-reduce | flops 2 | bytes 16 | tf_op jit(solution)/shard_map/psum | solution.py:43
  595.3 8.0 convolution_bitcast_fusion.11
  603.7 3.9 collective-permute-done.30
  607.8 5.2 collective-permute-done.31
  613.2 7.8 collective-permute-done.32
  621.1 11.7 collective-permute-start.33
  635.7 4.4 collective-permute-done.34
  640.2 3.4 convolution_bitcast_fusion.10
  645.4 60.2 %psum.62 = f32[2]{0:T(128)S(1)} all-reduce(f32[2]{0:T(128)S(1)} %get-tuple-element.41), channel_id=1, replica_groups=mesh['dom'=32,'load'=8] {'dom'}, use_global_device_ids=true, to_apply=%region_13.0 | all-reduce | flops 2 | bytes 16 | tf_op jit(solution)/shard_map/psum | solution.py:43
  706.0 8.0 convolution_bitcast_fusion.9
  718.4 5.0 collective-permute-done.36
  723.5 7.8 collective-permute-done.37
  731.4 11.8 collective-permute-start.38
  746.1 4.4 collective-permute-done.39
  750.5 3.4 convolution_bitcast_fusion.8
  755.8 62.0 %psum.63 = f32[2]{0:T(128)S(1)} all-reduce(f32[2]{0:T(128)S(1)} %fusion.21), channel_id=1, replica_groups=mesh['dom'=32,'load'=8] {'dom'}, use_global_device_ids=true, to_apply=%region_15.0 | all-reduce | flops 2 | bytes 16 | tf_op jit(solution)/shard_map/psum | solution.py:43
  817.9 90.5 %gather_fusion.3 = f32[16384]{0:T(1024)S(1)} fusion(f32[1536]{0:T(1024)S(1)} %bitcast.270, s32[16384]{0:T(1024)S(1)} %get-tuple-element.43), kind=kCustom, calls=%fused_computation.3 | custom fusion | bytes 196608 | tf_op jit(solution)/shard_map/gather | solution.py:97
  908.5 90.5 %gather_fusion.1 = f32[16384]{0:T(1024)S(1)} fusion(f32[1536]{0:T(1024)S(1)} %bitcast.272, s32[16384]{0:T(1024)S(1)} %get-tuple-element.43), kind=kCustom, calls=%fused_computation.1 | custom fusion | bytes 196608 | tf_op jit(solution)/shard_map/gather | solution.py:98
  999.0 90.5 %gather_fusion = f32[16384]{0:T(1024)S(1)} fusion(f32[1536]{0:T(1024)S(1)} %bitcast.273, s32[16384]{0:T(1024)S(1)} %get-tuple-element.44), kind=kCustom, calls=%fused_computation | custom fusion | bytes 196608 | tf_op jit(solution)/shard_map/gather | solution.py:98
  1089.5 90.5 %gather_fusion.2 = f32[16384]{0:T(1024)S(1)} fusion(f32[1536]{0:T(1024)S(1)} %bitcast.271, s32[16384]{0:T(1024)S(1)} %get-tuple-element.44), kind=kCustom, calls=%fused_computation.2 | custom fusion | bytes 196608 | tf_op jit(solution)/shard_map/gather | solution.py:97
  1180.7 13.6 %all-gather = f32[131072]{0:T(1024)S(1)} all-gather(f32[16384]{0:T(1024)S(1)} %multiply_negate_fusion), channel_id=2, replica_groups=mesh['dom'=32,'load'=8] {'load'}, dimensions={0}, use_global_device_ids=true | all-gather | bytes 589824 | tf_op jit(solution)/shard_map/all_gather | solution.py:100
  (226 shorter events, 74.5 us)
Async XLA Ops:
  0.6 12.6 %copy-start = (f32[12,128,128]{2,1,0:T(8,128)S(1)}, f32[12,128,128]{2,1,0:T(8,128)}, u32[]{:S(2)}) copy-start(f32[12,128,128]{2,1,0:T(8,128)} %param.13) | copy-start | bytes 2359300
  0.6 12.6 %copy-start.10 = (f32[1,1536]{1,0:T(1,128)S(1)}, f32[1,1536]{1,0:T(1,128)}, u32[]{:S(2)}) copy-start(f32[1,1536]{1,0:T(1,128)} %param.9) | copy-start | bytes 18436
  0.7 35.7 %copy-start.11 = (f32[1536]{0:T(1024)S(1)}, f32[1536]{0:T(1024)}, u32[]{:S(2)}) copy-start(f32[1536]{0:T(1024)} %param.11) | copy-start | bytes 18436
  1.4 38.1 %copy-start.1 = (f32[5,12,128,128]{3,2,1,0:T(8,128)S(1)}, f32[5,12,128,128]{3,2,1,0:T(8,128)}, u32[]{:S(2)}) copy-start(f32[5,12,128,128]{3,2,1,0:T(8,128)} %param.14) | copy-start | bytes 11796484
  3.4 39.5 %copy-start.9 = (s32[5,12]{1,0:T(8,128)S(1)}, s32[5,12]{1,0:T(8,128)}, u32[]{:S(2)}) copy-start(s32[5,12]{1,0:T(8,128)} %param.15) | copy-start | bytes 724
  3.4 39.5 %copy-start.14 = (f32[5]{0:T(128)S(1)}, f32[5]{0:T(128)}, u32[]{:S(2)}) copy-start(f32[5]{0:T(128)} %constant.32) | copy-start | bytes 64
  11.3 4.3 collective-permute-start
  15.6 5.4 collective-permute-start.1
  21.1 8.9 collective-permute-start.2
  30.0 3.9 collective-permute-start.3
  34.0 5.5 collective-permute-start.4
  42.9 33.2 %copy-start.8 = (f32[12,128,128]{2,1,0:T(8,128)S(1)}, f32[12,128,128]{2,1,0:T(8,128)}, u32[]{:S(2)}) copy-start(f32[12,128,128]{2,1,0:T(8,128)} %param.12) | copy-start | bytes 2359300
  44.8 37.5 %copy-start.13 = (f32[5]{0:T(128)S(1)}, f32[5]{0:T(128)}, u32[]{:S(2)}) copy-start(f32[5]{0:T(128)} %constant.25.clone) | copy-start | bytes 64
  51.0 4.2 collective-permute-start.5
  55.3 5.1 collective-permute-start.6
  60.5 8.9 collective-permute-start.7
  69.4 3.9 collective-permute-start.8
  73.4 5.5 collective-permute-start.9
  148.6 45.7 %copy-start.2 = (f32[5,12,128,128]{3,2,1,0:T(8,128)S(1)}, f32[5,12,128,128]{3,2,1,0:T(8,128)}, u32[]{:S(2)}) copy-start(f32[5,12,128,128]{3,2,1,0:T(8,128)} %param.14) | copy-start | bytes 11796484
  156.9 4.3 collective-permute-start.10
  161.2 5.1 collective-permute-start.11
  166.4 8.0 collective-permute-start.12
  174.4 14.2 %collective-permute-start.13 = (f32[2,2,12,128]{3,1,2,0:T(2,128)S(1)}, f32[2,2,12,128]{3,1,2,0:T(2,128)S(1)}, u32[]{:S(2)}, u32[]{:S(2)}) collective-permute-start(f32[2,2,12,128]{3,1,2,0:T(2,128)S(1)} %slice.305), channel_id=1, source_target_pairs={{0,64},{8,72},{16,80},{24,88},{32,96},{40,104},{48,112},{56,120},{... | collective-permute-start | bytes 73736 | tf_op jit(solution)/shard_map/ppermute | solution.py:14
  188.6 5.7 collective-permute-start.14
  259.7 45.1 %copy-start.3 = (f32[5,12,128,128]{3,2,1,0:T(8,128)S(1)}, f32[5,12,128,128]{3,2,1,0:T(8,128)}, u32[]{:S(2)}) copy-start(f32[5,12,128,128]{3,2,1,0:T(8,128)} %param.14) | copy-start | bytes 11796484
  268.0 4.3 collective-permute-start.15
  272.3 5.1 collective-permute-start.16
  277.5 8.0 collective-permute-start.17
  285.5 13.7 %collective-permute-start.18 = (f32[2,2,12,128]{3,1,2,0:T(2,128)S(1)}, f32[2,2,12,128]{3,1,2,0:T(2,128)S(1)}, u32[]{:S(2)}, u32[]{:S(2)}) collective-permute-start(f32[2,2,12,128]{3,1,2,0:T(2,128)S(1)} %slice.313), channel_id=1, source_target_pairs={{0,64},{8,72},{16,80},{24,88},{32,96},{40,104},{48,112},{56,120},{... | collective-permute-start | bytes 73736 | tf_op jit(solution)/shard_map/ppermute | solution.py:14
  299.3 5.5 collective-permute-start.19
  372.2 45.0 %copy-start.4 = (f32[5,12,128,128]{3,2,1,0:T(8,128)S(1)}, f32[5,12,128,128]{3,2,1,0:T(8,128)}, u32[]{:S(2)}) copy-start(f32[5,12,128,128]{3,2,1,0:T(8,128)} %param.14) | copy-start | bytes 11796484
  380.6 4.3 collective-permute-start.20
  384.9 5.1 collective-permute-start.21
  390.1 8.0 collective-permute-start.22
  398.1 13.5 %collective-permute-start.23 = (f32[2,2,12,128]{3,1,2,0:T(2,128)S(1)}, f32[2,2,12,128]{3,1,2,0:T(2,128)S(1)}, u32[]{:S(2)}, u32[]{:S(2)}) collective-permute-start(f32[2,2,12,128]{3,1,2,0:T(2,128)S(1)} %slice.321), channel_id=1, source_target_pairs={{0,64},{8,72},{16,80},{24,88},{32,96},{40,104},{48,112},{56,120},{... | collective-permute-start | bytes 73736 | tf_op jit(solution)/shard_map/ppermute | solution.py:14
  411.7 5.5 collective-permute-start.24
  482.6 45.5 %copy-start.5 = (f32[5,12,128,128]{3,2,1,0:T(8,128)S(1)}, f32[5,12,128,128]{3,2,1,0:T(8,128)}, u32[]{:S(2)}) copy-start(f32[5,12,128,128]{3,2,1,0:T(8,128)} %param.14) | copy-start | bytes 11796484
  491.0 4.3 collective-permute-start.25
  495.3 5.1 collective-permute-start.26
  500.4 8.0 collective-permute-start.27
  508.4 14.0 %collective-permute-start.28 = (f32[2,2,12,128]{3,1,2,0:T(2,128)S(1)}, f32[2,2,12,128]{3,1,2,0:T(2,128)S(1)}, u32[]{:S(2)}, u32[]{:S(2)}) collective-permute-start(f32[2,2,12,128]{3,1,2,0:T(2,128)S(1)} %slice.329), channel_id=1, source_target_pairs={{0,64},{8,72},{16,80},{24,88},{32,96},{40,104},{48,112},{56,120},{... | collective-permute-start | bytes 73736 | tf_op jit(solution)/shard_map/ppermute | solution.py:14
  522.4 5.7 collective-permute-start.29
  595.0 45.1 %copy-start.6 = (f32[5,12,128,128]{3,2,1,0:T(8,128)S(1)}, f32[5,12,128,128]{3,2,1,0:T(8,128)}, u32[]{:S(2)}) copy-start(f32[5,12,128,128]{3,2,1,0:T(8,128)} %param.14) | copy-start | bytes 11796484
  603.4 4.3 collective-permute-start.30
  607.7 5.4 collective-permute-start.31
  613.1 8.0 collective-permute-start.32
  621.1 13.6 %collective-permute-start.33 = (f32[2,2,12,128]{3,1,2,0:T(2,128)S(1)}, f32[2,2,12,128]{3,1,2,0:T(2,128)S(1)}, u32[]{:S(2)}, u32[]{:S(2)}) collective-permute-start(f32[2,2,12,128]{3,1,2,0:T(2,128)S(1)} %slice.337), channel_id=1, source_target_pairs={{0,64},{8,72},{16,80},{24,88},{32,96},{40,104},{48,112},{56,120},{... | collective-permute-start | bytes 73736 | tf_op jit(solution)/shard_map/ppermute | solution.py:14
  634.7 5.5 collective-permute-start.34
  640.2 75.6 %copy-start.12 = (s32[2,16384]{1,0:T(2,128)S(1)}, s32[2,16384]{1,0:T(2,128)}, u32[]{:S(2)}) copy-start(s32[2,16384]{1,0:T(2,128)} %param.16) | copy-start | bytes 393220
  705.6 44.9 %copy-start.7 = (f32[5,12,128,128]{3,2,1,0:T(8,128)S(1)}, f32[5,12,128,128]{3,2,1,0:T(8,128)}, u32[]{:S(2)}) copy-start(f32[5,12,128,128]{3,2,1,0:T(8,128)} %param.14) | copy-start | bytes 11796484
  714.0 4.3 collective-permute-start.35
  718.3 5.1 collective-permute-start.36
  723.4 8.0 collective-permute-start.37
  731.4 13.6 %collective-permute-start.38 = (f32[2,2,12,128]{3,1,2,0:T(2,128)S(1)}, f32[2,2,12,128]{3,1,2,0:T(2,128)S(1)}, u32[]{:S(2)}, u32[]{:S(2)}) collective-permute-start(f32[2,2,12,128]{3,1,2,0:T(2,128)S(1)} %slice.345), channel_id=1, source_target_pairs={{0,64},{8,72},{16,80},{24,88},{32,96},{40,104},{48,112},{56,120},{... | collective-permute-start | bytes 73736 | tf_op jit(solution)/shard_map/ppermute | solution.py:14
  745.0 5.5 collective-permute-start.39
